TPU v7x, 128 devices: a whole 4x4x4 slice. The times are simulated.
128 devices in a mesh: row: 16 (over y, z), basis: 8 (over x, core).
Axes of the slice: x: 4, y: 4, z: 4, core: 2. Of those that a mesh axis runs over, the one named last changes fastest.
Arguments:
- design: float32 [15360, 40960], P('row', 'basis'), may hold values from -0.029646354 to 0.029646354
- targets: float32 [15360], P('row'), may hold values from -6 to 6
- counts: int32 [15360, 128], P('row'), may hold values from 0 to 3
- coefficients: float32 [40960, 128], P('basis'), may hold values from -6 to 6
- step_size: float32 [128], replicated, may hold values from 0.03 to 0.15
Outputs:
- fitted: float32 [40960, 128], P('basis')
- influence: float32 [15360, 128], P('row')
All inputs are finite; a program needn't handle non-finite values.
Results may differ from a plain program's by a relative error of at most 0.00017.
Values sent between devices are 32-bit elements; how exact they have to be, the bound alone decides.
A program may use at most 128 MiB of HBM per device.

v0:
```python
import jax
import jax.numpy as jnp
from jax import lax
from jax.sharding import PartitionSpec as P

STEPS = 3


HIGH = lax.Precision.HIGHEST


def gathered_total(x, axis):
    return lax.all_gather(x, axis).sum(0)


def cut_along(x, dim, peers):
    before, after = (x.shape[:dim], x.shape[dim + 1 :])
    return jnp.moveaxis(x.reshape(*before, peers, -1, *after), dim, 0)


def sent_and_summed(x, axis, dim):
    peers = lax.axis_size(axis)
    blocks = lax.all_to_all(cut_along(x, dim, peers), axis, 0, 0, tiled=True)
    return jnp.sum(blocks, axis=0)


def laid_out(blocks, dim):
    blocks = jnp.moveaxis(blocks, 0, dim)
    lengths = blocks.shape
    return blocks.reshape(*lengths[:dim], lengths[dim] * lengths[dim + 1], *lengths[dim + 2 :])


def copy_for_each(x, axis):
    copies = jnp.broadcast_to(x, (lax.axis_size(axis), *x.shape))
    return lax.all_to_all(copies, axis, split_axis=0, concat_axis=0, tiled=True)


def gather_directly(x, axis, dim):
    return laid_out(copy_for_each(x, axis), dim)


def transposed(left, right):
    return lax.dot_general(
        left, right, (((0,), (0,)), ((), ())), precision=HIGH, preferred_element_type=jnp.float32
    )


def predictions(partial_value):
    return gathered_total(partial_value, "basis")


def weighted(predicted, targets, weights):
    residual = predicted - targets[:, None]
    return weights * residual / jnp.sqrt(1.0 + residual * residual)


def shards(design, targets, counts, coefficients, step_size):
    weights = counts.astype(jnp.float32)
    curve_term = transposed(design * design, weights)
    influence = jnp.zeros((design.shape[0], coefficients.shape[1]), jnp.float32)
    share_rows = coefficients.shape[0] // lax.axis_size("row")
    offset = lax.axis_index("row") * share_rows
    curvature = sent_and_summed(curve_term, "row", 0) + 0.01
    share = lax.dynamic_slice_in_dim(coefficients, offset, share_rows, 0)
    for step in range(STEPS):
        if step == 0:
            partial_value = jnp.dot(
                design, coefficients, precision=HIGH, preferred_element_type=jnp.float32
            )
        else:
            partial_value = jnp.dot(
                design,
                gather_directly(share, "row", 0),
                precision=HIGH,
                preferred_element_type=jnp.float32,
            )
        influence = weighted(predictions(partial_value), targets, weights)
        gradient = sent_and_summed(transposed(design, influence), "row", 0)
        share = share - step_size[None, :] * gradient / curvature
    fitted = gather_directly(share, "row", 0)
    return (fitted, influence)


def solution(mesh):
    return jax.shard_map(
        shards,
        mesh=mesh,
        in_specs=(P("row", "basis"), P("row"), P("row", None), P("basis", None), P()),
        out_specs=(P("basis", None), P("row", None)),
        check_vma=False,
    )
```

profile of v0, /device:TPU:0, one launch (start us, length us, event | category | flops | bytes accessed | tf_op | source)
XLA Modules:
  0.0 485.2 jit_solution(1836256925751249367)
XLA Ops:
  7.2 0.0 all-gather.7.cloned.1.call-start
  7.2 19.3 %fusion.23 = f32[960,128]{1,0:T(8,128)} fusion(f32[960,5120]{1,0:T(8,128)} %param.5, f32[5120,128]{1,0:T(8,128)} %param.8), kind=kOutput, calls=%fused_computation.32 | convolution fusion | flops 7549747200 | bytes 22773760 | tf_op jit(solution)/shard_map/dot_general | solution.py:67
  26.5 0.0 all-gather.7.cloned.1.call-update
  26.6 36.7 %fusion = f32[5120,128]{1,0:T(8,128)} fusion(f32[960,5120]{1,0:T(8,128)} %param.5, s32[960,128]{1,0:T(8,128)S(1)} %copy-done), kind=kOutput, calls=%fused_computation | convolution fusion | flops 7554785280 | bytes 22773760 | tf_op jit(solution)/shard_map/dot_general | solution.py:43
  63.3 8.2 %all-to-all-start.1 = ((f32[16,320,128]{2,1,0:T(8,128)}), f32[16,320,128]{2,1,0:T(8,128)}, u32[]{:S(2)}, u32[]{:S(2)}) async-start(f32[16,320,128]{2,1,0:T(8,128)} %bitcast.3), calls=%async_computation.1 | async-start | bytes 5242880 | tf_op jit(solution)/shard_map/all_to_all | solution.py:23
  71.5 0.0 copy-start.4
  71.5 0.0 all-gather.7.cloned.1.call-done
  71.5 3.1 reduce_sum.63
  74.7 0.0 copy-done.4
  74.7 14.2 %convolution_bitcast_fusion.2 = f32[5120,128]{0,1:T(8,128)S(1)} fusion(f32[960,5120]{1,0:T(8,128)} %param.5, f32[960,128]{1,0:T(8,128)} %reduce_sum.63, s32[960,128]{1,0:T(8,128)S(1)} %copy-done, f32[960]{0:T(1024)S(1)} %copy-done.4), kind=kOutput, calls=%fused_computation.4 | convolution fusion | flops 7550484480 | bytes 23269120 | tf_op jit(solution)/shard_map/dot_general | solution.py:43
  88.9 2.1 copy.7
  91.0 17.6 %all-to-all-done.1 = f32[16,320,128]{2,1,0:T(8,128)} async-done(((f32[16,320,128]{2,1,0:T(8,128)}), f32[16,320,128]{2,1,0:T(8,128)}, u32[]{:S(2)}, u32[]{:S(2)}) %all-to-all-start.1) | async-done | bytes 2621472 | tf_op jit(solution)/shard_map/all_to_all | solution.py:23
  108.6 4.2 all-to-all-start
  112.9 0.0 all-gather.9.cloned.1.call-start
  112.9 0.0 copy-start.5
  112.9 1.9 reduce_sum.65
  114.8 32.2 %all-to-all-done = f32[16,320,128]{2,1,0:T(8,128)S(1)} async-done(((f32[16,320,128]{2,1,0:T(8,128)}), f32[16,320,128]{2,1,0:T(8,128)S(1)}, u32[]{:S(2)}, u32[]{:S(2)}) %all-to-all-start) | async-done | bytes 2621472 | tf_op jit(solution)/shard_map/all_to_all | solution.py:23
  147.0 0.8 reduce_sum.64
  147.8 1.0 divide_subtract_fusion.2
  148.8 0.2 broadcast_in_dim.6
  149.1 35.2 %all_to_all.35 = f32[16,320,128]{2,1,0:T(8,128)S(1)} all-to-all(f32[16,320,128]{2,1,0:T(8,128)S(1)} %broadcast_in_dim.6), channel_id=1, replica_groups=mesh['row'=16,'basis'=8] {'row'}, dimensions={0} | all-to-all | bytes 5242880 | tf_op jit(solution)/shard_map/all_to_all | solution.py:35
  184.2 19.2 %convolution_bitcast_fusion.4 = f32[960,128]{1,0:T(8,128)} fusion(f32[5120,128]{1,0:T(8,128)S(1)} %bitcast.30, f32[960,5120]{1,0:T(8,128)} %param.5), kind=kOutput, calls=%fused_computation.6 | convolution fusion | flops 7549747200 | bytes 22773760 | tf_op jit(solution)/shard_map/dot_general | solution.py:71
  203.4 0.0 all-gather.9.cloned.1.call-update
  203.4 0.0 all-gather.11.cloned.1.call-start
  203.5 29.3 %all-gather.9.cloned.1.call-done = f32[7680,128]{1,0:T(8,128)} async-done(((f32[960,128]{1,0:T(8,128)}), f32[7680,128]{1,0:T(8,128)}) %all-gather.9.cloned.1.call-update) | async-done | bytes 3932176 | tf_op jit(solution)/shard_map/all_gather | solution.py:13
  232.8 3.1 reduce_sum.66
  235.9 14.2 %convolution_bitcast_fusion.1 = f32[5120,128]{0,1:T(8,128)S(1)} fusion(f32[960,5120]{1,0:T(8,128)} %param.5, f32[960,128]{1,0:T(8,128)} %reduce_sum.66, s32[960,128]{1,0:T(8,128)S(1)} %copy-done, f32[960]{0:T(1024)S(1)} %copy-done.4), kind=kOutput, calls=%fused_computation.3 | convolution fusion | flops 7550484480 | bytes 23269120 | tf_op jit(solution)/shard_map/dot_general | solution.py:43
  250.2 2.1 copy.8
  252.2 41.4 %all_to_all.36 = f32[16,320,128]{2,1,0:T(8,128)S(1)} all-to-all(f32[16,320,128]{2,1,0:T(8,128)} %bitcast.33), channel_id=1, replica_groups=mesh['row'=16,'basis'=8] {'row'}, dimensions={0} | all-to-all | bytes 5242880 | tf_op jit(solution)/shard_map/all_to_all | solution.py:23
  293.6 0.8 reduce_sum.67
  294.4 0.9 divide_subtract_fusion.1
  295.4 0.2 broadcast_in_dim.7
  295.6 36.5 %all_to_all.37 = f32[16,320,128]{2,1,0:T(8,128)S(1)} all-to-all(f32[16,320,128]{2,1,0:T(8,128)S(1)} %broadcast_in_dim.7), channel_id=1, replica_groups=mesh['row'=16,'basis'=8] {'row'}, dimensions={0} | all-to-all | bytes 5242880 | tf_op jit(solution)/shard_map/all_to_all | solution.py:35
  332.1 19.1 %convolution_bitcast_fusion.3 = f32[960,128]{1,0:T(8,128)} fusion(f32[5120,128]{1,0:T(8,128)S(1)} %bitcast.31, f32[960,5120]{1,0:T(8,128)} %param.5), kind=kOutput, calls=%fused_computation.5 | convolution fusion | flops 7549747200 | bytes 22773760 | tf_op jit(solution)/shard_map/dot_general | solution.py:71
  351.2 0.0 all-gather.11.cloned.1.call-update
  351.3 27.6 %all-gather.11.cloned.1.call-done = f32[7680,128]{1,0:T(8,128)} async-done(((f32[960,128]{1,0:T(8,128)}), f32[7680,128]{1,0:T(8,128)}) %all-gather.11.cloned.1.call-update) | async-done | bytes 3932176 | tf_op jit(solution)/shard_map/all_gather | solution.py:13
  378.8 2.4 reduce_sum.68
  381.2 0.2 rsqrt_multiply_fusion
  381.4 0.0 copy-start.1
  381.4 0.8 copy-done.1
  382.2 13.8 %convolution_bitcast_fusion = f32[5120,128]{0,1:T(8,128)S(1)} fusion(f32[960,128]{1,0:T(8,128)S(1)} %rsqrt_multiply_fusion, f32[960,5120]{1,0:T(8,128)} %param.5), kind=kOutput, calls=%fused_computation.2 | convolution fusion | flops 7549747200 | bytes 22773760 | tf_op jit(solution)/shard_map/dot_general | solution.py:43
  396.0 2.1 copy.9
  398.1 41.4 %all_to_all.38 = f32[16,320,128]{2,1,0:T(8,128)S(1)} all-to-all(f32[16,320,128]{2,1,0:T(8,128)} %bitcast.34), channel_id=1, replica_groups=mesh['row'=16,'basis'=8] {'row'}, dimensions={0} | all-to-all | bytes 5242880 | tf_op jit(solution)/shard_map/all_to_all | solution.py:23
  439.5 0.1 reduce_sum.69
  439.6 0.8 copy-done.3
  440.4 0.2 broadcast_in_dim.8
  440.7 36.5 %all_to_all.39 = f32[16,320,128]{2,1,0:T(8,128)S(1)} all-to-all(f32[16,320,128]{2,1,0:T(8,128)S(1)} %broadcast_in_dim.8), channel_id=1, replica_groups=mesh['row'=16,'basis'=8] {'row'}, dimensions={0} | all-to-all | bytes 5242880 | tf_op jit(solution)/shard_map/all_to_all | solution.py:35
  477.2 1.5 copy.11
  (7 shorter events, 0.0 us)
Async XLA Ops:
  7.2 19.4 %copy-start = (s32[960,128]{1,0:T(8,128)S(1)}, s32[960,128]{1,0:T(8,128)}, u32[]{:S(2)}) copy-start(s32[960,128]{1,0:T(8,128)} %param.7) | copy-start | bytes 1474564
  7.2 64.4 %all-gather.7.cloned.1.call-start = ((), (), s32[]{:S(2)}) async-start(), calls=%async_computation.7 | async-start | bytes 4423680 | tf_op jit(solution)/shard_map/all_gather | solution.py:13
  63.3 45.3 %all-to-all-start.1 = ((f32[16,320,128]{2,1,0:T(8,128)}), f32[16,320,128]{2,1,0:T(8,128)}, u32[]{:S(2)}, u32[]{:S(2)}) async-start(f32[16,320,128]{2,1,0:T(8,128)} %bitcast.3), calls=%async_computation.1 | async-start | bytes 5242880 | tf_op jit(solution)/shard_map/all_to_all | solution.py:23
  71.5 3.2 copy-start.4
  108.6 38.4 %all-to-all-start = ((f32[16,320,128]{2,1,0:T(8,128)}), f32[16,320,128]{2,1,0:T(8,128)S(1)}, u32[]{:S(2)}, u32[]{:S(2)}) async-start(f32[16,320,128]{2,1,0:T(8,128)} %bitcast.32), calls=%async_computation | async-start | bytes 5242880 | tf_op jit(solution)/shard_map/all_to_all | solution.py:23
  112.9 119.9 %all-gather.9.cloned.1.call-start = ((), (), s32[]{:S(2)}) async-start(), calls=%async_computation.8 | async-start | bytes 4423680 | tf_op jit(solution)/shard_map/all_gather | solution.py:13
  112.9 34.9 %copy-start.5 = (f32[128]{0:T(128)S(1)}, f32[128]{0:T(128)}, u32[]{:S(2)}) copy-start(f32[128]{0:T(128)} %param.9) | copy-start | bytes 1540
  203.4 175.4 %all-gather.11.cloned.1.call-start = ((), (), s32[]{:S(2)}) async-start(), calls=%async_computation.9 | async-start | bytes 4423680 | tf_op jit(solution)/shard_map/all_gather | solution.py:13
  295.3 36.8 %copy-start.2 = (f32[320,128]{1,0:T(8,128)}, f32[320,128]{1,0:T(8,128)S(1)}, u32[]{:S(2)}) copy-start(f32[320,128]{1,0:T(8,128)S(1)} %divide_subtract_fusion.1) | copy-start | bytes 491524
  381.4 0.8 copy-start.1
  439.5 0.9 copy-start.3
Sparse Core Ops, SparseCore 0:
  26.7 33.4 all-gather.6
  203.5 29.1 all-gather.8
  351.4 27.3 all-gather.10
where the time goes:
time: 486 us; the launch traced here: 485 us
  blocking collectives  191 us (39%)
  matrix products  137 us (28%)
  waiting for transfers between devices  107 us (22%)
  other arithmetic  14.4 us (3%)
  between operations  13.9 us (3%)
  starting transfers between devices  12.5 us (3%)
  local copies, waits for them, and re-layouts  10.1 us (2%)
    all_to_all x3, blocking collectives, copy_for_each(): return lax.all_to_all(copies, axis, split_axis=0, concat_axis=0, tiled=True)  108 us
    all_to_all x2, blocking collectives, sent_and_summed(): blocks = lax.all_to_all(cut_along(x, dim, peers), axis, 0, 0, tiled=True)  82.7 us
    dot_general x4, matrix products, transposed(): lax.dot_general(left, right, (((0,), (0,)), ((), ())), precision=HIGH, pr...  79.1 us
    all_gather x3, waiting for transfers between devices, gathered_total(): return lax.all_gather(x, axis).sum(0)  56.9 us
    all_to_all x2, waiting for transfers between devices, sent_and_summed(): blocks = lax.all_to_all(cut_along(x, dim, peers), axis, 0, 0, tiled=True)  49.8 us
    dot_general x2, matrix products, shards(): jnp.dot(design, gather_directly(share, 'row', 0), precision=HIGH, preferr...  38.3 us
    dot_general x1, matrix products, shards(): jnp.dot(design, coefficients, precision=HIGH, preferred_element_type=jnp....  19.3 us
    all_to_all x2, starting transfers between devices, sent_and_summed(): blocks = lax.all_to_all(cut_along(x, dim, peers), axis, 0, 0, tiled=True)  12.4 us
  transfers between devices with their start and end apart: 5, of which 4 were waited for; matrix products, arithmetic and copies ran while one was open for 12% of the time, Pallas kernels for 0%

commit v1 on v0

v1 whole, which is shorter than its diff:
```python
import functools

import jax
import jax.numpy as jnp
from jax import lax
from jax.experimental import pallas as pl
from jax.experimental.pallas import tpu as pltpu
from jax.sharding import PartitionSpec as P

STEPS = 3
SIDE = 4
LOADS = 10
GROUPS = 2
MESH = pl.DeviceIdType.MESH
F32 = jnp.float32
BF16 = jnp.bfloat16


def dot(a, b, ca=1, cb=0):
    return lax.dot_general(a, b, (((ca,), (cb,)), ((), ())), preferred_element_type=F32)


def parts(x):
    high = x.astype(BF16)
    return high, (x - high.astype(F32)).astype(BF16)


def kernel(
    design, coef, counts, targets, step_size, fit_out, inf_out,
    raw, dh, dl, cin, kin, wt, wtb, acc, curve, icat,
    grad, fit, infl, pred, r1, s1, r2, r3, rate, c1, sc, c2,
    load_sem, in_sem, out_sem,
    p1s, p1r, p2s, p2r, p3s, p3r, p4s, p4r, x1s, x1r, x2s, x2r, k1s, k1r, k2s, k2r,
):
    rows, cols = raw.shape
    members = wt.shape[0]
    m = members // GROUPS
    quarter = cols // (2 * SIDE)
    half = cols // 2
    part = m // SIDE
    peers = lax.axis_size("basis")
    piece = m // peers
    row, me = lax.axis_index("row"), lax.axis_index("basis")
    y, z = row // SIDE, lax.rem(row, SIDE)

    def at_y(d):
        return (lax.rem(y + d, SIDE) * SIDE + z, me)

    def at_z(d):
        return (y * SIDE + lax.rem(z + d, SIDE), me)

    def at_b(k):
        return (row, lax.rem(me + k, peers))

    first, second = (at_y, at_z), (at_z, at_y)
    major, minor = (y, z), (z, y)

    def columns(h, q):
        return pl.ds(pl.multiple_of(h * half + q * quarter, 128), quarter)

    def share_rows(h, d=0):
        return pl.ds(pl.multiple_of(lax.rem(minor[h] + d, SIDE) * part, 8), part)

    def piece_rows(k=0):
        return pl.ds(pl.multiple_of(lax.rem(me + k, peers) * piece, 8), piece)

    def remote(src, dst, send, recv, to):
        return pltpu.make_async_remote_copy(
            src_ref=src, dst_ref=dst, send_sem=send, recv_sem=recv, device_id=to, device_id_type=MESH
        )

    width = cols // LOADS

    def load(i):
        c = pl.ds(pl.multiple_of(i * width, 128), width)
        return pltpu.make_async_copy(design.at[:, c], raw.at[:, c], load_sem.at[i])

    coef_in = pltpu.make_async_copy(coef, cin, in_sem.at[0])
    counts_in = pltpu.make_async_copy(counts, kin, in_sem.at[1])
    counts_in.start()
    coef_in.start()
    for i in range(LOADS):
        load(i).start()

    barrier = pltpu.get_barrier_semaphore()
    for d in range(1, SIDE):
        pl.semaphore_signal(barrier, inc=1, device_id=at_y(d), device_id_type=MESH)
        pl.semaphore_signal(barrier, inc=1, device_id=at_z(d), device_id_type=MESH)
    for k in range(1, peers):
        pl.semaphore_signal(barrier, inc=1, device_id=at_b(k), device_id_type=MESH)

    def send1(g, h, d):
        there = lax.rem(major[h] + d, SIDE)
        return remote(
            grad.at[g, :, columns(h, there)], r1.at[g, h, d - 1],
            p1s.at[g, h, d - 1], p1r.at[g, h, d - 1], first[h](d),
        )

    def send2(g, h, d):
        return remote(
            s1.at[g, h, share_rows(h, d)], r2.at[g, h, d - 1],
            p2s.at[g, h, d - 1], p2r.at[g, h, d - 1], second[h](d),
        )

    def send3(g, h, d):
        mine = fit.at[g, share_rows(h), columns(h, major[h])]
        return remote(mine, mine, p3s.at[g, h, d - 1], p3r.at[g, h, d - 1], second[h](d))

    def send4(g, h, d):
        mine = fit.at[g, :, columns(h, major[h])]
        return remote(mine, mine, p4s.at[g, h, d - 1], p4r.at[g, h, d - 1], first[h](d))

    def sendx1(g, k):
        return remote(
            pred.at[g, piece_rows(k)], r3.at[g, k - 1], x1s.at[g, k - 1], x1r.at[g, k - 1], at_b(k)
        )

    def sendx2(g, k):
        mine = infl.at[g, piece_rows()]
        return remote(mine, mine, x2s.at[g, k - 1], x2r.at[g, k - 1], at_b(k))

    def sendk1(h, d):
        there = lax.rem(major[h] + d, SIDE)
        return remote(
            curve.at[:, columns(h, there)], c1.at[h, d - 1],
            k1s.at[h, d - 1], k1r.at[h, d - 1], first[h](d),
        )

    def sendk2(h, d):
        return remote(
            sc.at[h, :, share_rows(h, d)], c2.at[h, d - 1],
            k2s.at[h, d - 1], k2r.at[h, d - 1], second[h](d),
        )

    def gradients(g):
        high, low = parts(infl[g])
        icat[0:m] = high
        icat[m:] = low

        def body(j, _):
            d = lax.rem(j + 1, SIDE)
            for h in range(2):
                c = columns(h, lax.rem(major[h] + d, SIDE))
                both = dot(icat[...], dh[:, c])
                grad[g, :, c] = both[:m] + both[m:] + dot(icat[0:m], dl[:, c])

            @pl.when(j < SIDE - 1)
            def _():
                for h in range(2):
                    send1(g, h, j + 1).start()

            return 0

        lax.fori_loop(0, SIDE, body, 0)

    def reduce1(g):
        for h in range(2):
            for d in range(1, SIDE):
                send1(g, h, d).wait_recv()
            s1[g, h] = (grad[g, :, columns(h, major[h])] + r1[g, h, 0]) + (r1[g, h, 1] + r1[g, h, 2])
            for d in range(1, SIDE):
                send2(g, h, d).start()
        for h in range(2):
            for d in range(1, SIDE):
                send1(g, h, d).wait_send()

    def update(g):
        for h in range(2):
            for d in range(1, SIDE):
                send2(g, h, d).wait_recv()
            total = (s1[g, h, share_rows(h)] + r2[g, h, 0]) + (r2[g, h, 1] + r2[g, h, 2])
            c = columns(h, major[h])
            fit[g, share_rows(h), c] = fit[g, share_rows(h), c] - total * rate[g, h]
            for d in range(1, SIDE):
                send3(g, h, d).start()
        for h in range(2):
            for d in range(1, SIDE):
                send2(g, h, d).wait_send()

    def spread(g):
        for h in range(2):
            for d in range(1, SIDE):
                send3(g, h, d).wait_recv()
            for d in range(1, SIDE):
                send4(g, h, d).start()
        for h in range(2):
            for d in range(1, SIDE):
                send3(g, h, d).wait_send()

    def predict(g, d):
        total = None
        for h in range(2):
            c = columns(h, lax.rem(major[h] + SIDE - d, SIDE))
            high, low = parts(fit[g, :, c])
            both = dot(jnp.concatenate([high, low], 0), dh[:, c], 1, 1)
            term = both[:m] + both[m:] + dot(high, dl[:, c], 1, 1)
            total = term if total is None else total + term
        return total

    def predict_own(g):
        pred[g] = predict(g, 0)

    def predict_rest(g):
        def body(d, _):
            for h in range(2):
                send4(g, h, d).wait_recv()
            pred[g] += predict(g, d)
            return 0

        lax.fori_loop(1, SIDE, body, 0)
        for h in range(2):
            for d in range(1, SIDE):
                send4(g, h, d).wait_send()

    def scatter_pred(g):
        for k in range(1, peers):
            sendx1(g, k).start()

    def influence(g):
        for k in range(1, peers):
            sendx1(g, k).wait_recv()
        total = pred[g, piece_rows()]
        for k in range(1, peers):
            total = total + r3[g, k - 1]
        residual = total - targets[...]
        w = wt[pl.ds(pl.multiple_of(g * m + me * piece, 8), piece)]
        infl[g, piece_rows()] = w * residual / jnp.sqrt(1.0 + residual * residual)
        for k in range(1, peers):
            sendx2(g, k).start()
        for k in range(1, peers):
            sendx1(g, k).wait_send()

    def gathered(g):
        for k in range(1, peers):
            sendx2(g, k).wait_recv()
        for k in range(1, peers):
            sendx2(g, k).wait_send()

    counts_in.wait()
    wt[...] = kin[...].astype(F32).T
    wtb[...] = wt[...].astype(BF16)
    coef_in.wait()
    acc[...] = jnp.zeros_like(acc)

    def first_chunk(i, _):
        load(i).wait()
        c = pl.ds(pl.multiple_of(i * width, 128), width)
        high, low = parts(raw[:, c])
        dh[:, c] = high
        dl[:, c] = low
        fh, fl = parts(cin[c, :])
        both = dot(high, jnp.concatenate([fh, fl], 1))
        acc[...] += both[:, :members] + both[:, members:] + dot(low, fh)
        return 0

    lax.fori_loop(0, LOADS, first_chunk, 0)
    flipped = acc[...].T
    for g in range(GROUPS):
        pred[g] = flipped[g * m : (g + 1) * m]
    pl.semaphore_wait(barrier, 2 * (SIDE - 1) + peers - 1)
    for g in range(GROUPS):
        scatter_pred(g)

    def curve_chunk(j, _):
        d = lax.rem(j + 1, SIDE)
        for h in range(2):
            c = columns(h, lax.rem(major[h] + d, SIDE))
            x = raw[:, c]
            high, low = parts(x * x)
            curve[:, c] = dot(wtb[...], high) + dot(wtb[...], low)

        @pl.when(j < SIDE - 1)
        def _():
            for h in range(2):
                sendk1(h, j + 1).start()

        return 0

    lax.fori_loop(0, 2, curve_chunk, 0)
    influence(0)
    lax.fori_loop(2, SIDE, curve_chunk, 0)
    for h in range(2):
        start = pl.multiple_of(h * half + major[h] * quarter, 128)
        own = cin[pl.ds(start, quarter), :].T
        for g in range(GROUPS):
            fit[g, :, columns(h, major[h])] = own[g * m : (g + 1) * m]

    def curve_sum():
        for h in range(2):
            for d in range(1, SIDE):
                sendk1(h, d).wait_recv()
            total = (curve[:, columns(h, major[h])] + c1[h, 0]) + (c1[h, 1] + c1[h, 2])
            for g in range(GROUPS):
                sc[h, g] = total[g * m : (g + 1) * m]
            for d in range(1, SIDE):
                sendk2(h, d).start()

    def curve_rate():
        for h in range(2):
            for d in range(1, SIDE):
                sendk2(h, d).wait_recv()
            for g in range(GROUPS):
                total = (sc[h, g, share_rows(h)] + c2[h, 0, g]) + (c2[h, 1, g] + c2[h, 2, g])
                mine = pl.ds(pl.multiple_of(g * m + minor[h] * part, 8), part)
                rate[g, h] = step_size[mine] / (total + 0.01)
        for h in range(2):
            for d in range(1, SIDE):
                sendk1(h, d).wait_send()
                sendk2(h, d).wait_send()

    def step(s, _):
        more = s < STEPS - 1
        gathered(0)
        gradients(0)
        pl.when(s == 0)(curve_sum)
        influence(1)
        reduce1(0)
        gathered(1)
        gradients(1)
        pl.when(s == 0)(curve_rate)
        update(0)
        spread(0)
        reduce1(1)
        pl.when(more)(lambda: predict_own(0))
        update(1)

        @pl.when(more)
        def _():
            predict_rest(0)
            scatter_pred(0)

        spread(1)

        @pl.when(more)
        def _():
            predict_own(1)
            influence(0)
            predict_rest(1)
            scatter_pred(1)

        return 0

    lax.fori_loop(0, STEPS, step, 0)

    inf_copy = pltpu.make_async_copy(infl, inf_out, in_sem.at[0])
    inf_copy.start()

    def out_copy(g, h, d):
        c = columns(h, lax.rem(major[h] + SIDE - d, SIDE))
        return pltpu.make_async_copy(fit.at[g, :, c], fit_out.at[g, :, c], out_sem.at[g, h, d])

    for g in range(GROUPS):
        for h in range(2):
            out_copy(g, h, 0).start()
            for d in range(1, SIDE):
                send4(g, h, d).wait_recv()
                out_copy(g, h, d).start()
    for g in range(GROUPS):
        for h in range(2):
            for d in range(1, SIDE):
                send4(g, h, d).wait_send()
            for d in range(SIDE):
                out_copy(g, h, d).wait()
    inf_copy.wait()


def shards(design, targets, counts, coefficients, step_size):
    rows, cols = design.shape
    members = coefficients.shape[1]
    m = members // GROUPS
    quarter = cols // (2 * SIDE)
    part = m // SIDE
    peers = lax.axis_size("basis")
    piece = m // peers
    vmem = pltpu.VMEM
    dma = pltpu.SemaphoreType.DMA
    gh = (GROUPS, 2, SIDE - 1)
    any_spec = pl.BlockSpec(memory_space=pl.ANY)
    vmem_spec = pl.BlockSpec(memory_space=pltpu.VMEM)
    fit, infl = pl.pallas_call(
        kernel,
        out_shape=(
            jax.ShapeDtypeStruct((GROUPS, m, cols), F32),
            jax.ShapeDtypeStruct((GROUPS, m, rows), F32),
        ),
        in_specs=[any_spec, any_spec, any_spec, vmem_spec, vmem_spec],
        out_specs=(any_spec, any_spec),
        scratch_shapes=[
            vmem((rows, cols), F32),
            vmem((rows, cols), BF16),
            vmem((rows, cols), BF16),
            vmem((cols, members), F32),
            vmem((rows, members), jnp.int32),
            vmem((members, rows), F32),
            vmem((members, rows), BF16),
            vmem((rows, members), F32),
            vmem((members, cols), F32),
            vmem((2 * m, rows), BF16),
            vmem((GROUPS, m, cols), F32),
            vmem((GROUPS, m, cols), F32),
            vmem((GROUPS, m, rows), F32),
            vmem((GROUPS, m, rows), F32),
            vmem((*gh, m, quarter), F32),
            vmem((GROUPS, 2, m, quarter), F32),
            vmem((*gh, part, quarter), F32),
            vmem((GROUPS, peers - 1, piece, rows), F32),
            vmem((GROUPS, 2, part, quarter), F32),
            vmem((2, SIDE - 1, members, quarter), F32),
            vmem((2, GROUPS, m, quarter), F32),
            vmem((2, SIDE - 1, GROUPS, part, quarter), F32),
            dma((LOADS,)),
            dma((2,)),
            dma((GROUPS, 2, SIDE)),
            *[dma(gh) for _ in range(8)],
            *[dma((GROUPS, peers - 1)) for _ in range(4)],
            *[dma((2, SIDE - 1)) for _ in range(4)],
        ],
        compiler_params=pltpu.CompilerParams(
            collective_id=0, has_side_effects=True, vmem_limit_bytes=60 * 2**20
        ),
    )(design, coefficients, counts, targets[None, :], step_size[:, None])
    return fit.reshape(members, cols).T, infl.reshape(members, rows).T


def solution(mesh):
    return jax.shard_map(
        shards,
        mesh=mesh,
        in_specs=(P("row", "basis"), P("row"), P("row", None), P("basis", None), P()),
        out_specs=(P("basis", None), P("row", None)),
        check_vma=False,
    )
```

time: 486 us -> 199 us (0.41)
  Pallas kernels: 0 us -> 192 us
  blocking collectives: 191 us -> 0 us
  matrix products: 137 us -> 0 us
  waiting for transfers between devices: 107 us -> 0 us
  other arithmetic: 14.4 us -> 0 us
  between operations: 13.9 us -> 0.65 us
  starting transfers between devices: 12.5 us -> 0 us
    pallas_call x0 -> x1, Pallas kernels: none -> 192 us  [shards(): pl.pallas_call(kernel, out_shape=(jax.ShapeDtypeStruct((GROUPS, m, cols),...]
    all_to_all x5 -> x0, blocking collectives: 191 us -> none  [the longest x3 108 us: copy_for_each(): return lax.all_to_all(copies, axis, split_axis=0, concat_axis=0, tiled=True)]
    dot_general x7 -> x0, matrix products: 137 us -> none  [the longest x4 79.1 us: transposed(): lax.dot_general(left, right, (((0,), (0,)), ((), ())), precision=HIGH, pr...]
    all_gather x3 -> x0, waiting for transfers between devices: 56.9 us -> none  [gathered_total(): return lax.all_gather(x, axis).sum(0)]
    all_to_all x2 -> x0, waiting for transfers between devices: 49.8 us -> none  [sent_and_summed(): blocks = lax.all_to_all(cut_along(x, dim, peers), axis, 0, 0, tiled=True)]
    all_to_all x2 -> x0, starting transfers between devices: 12.4 us -> none  [sent_and_summed(): blocks = lax.all_to_all(cut_along(x, dim, peers), axis, 0, 0, tiled=True)]
    reduce_sum x7 -> x0, other arithmetic: 12.2 us -> none  [the longest x3 8.62 us: gathered_total(): return lax.all_gather(x, axis).sum(0)]
    dot_general x3 -> x0, local copies, waits for them, and re-layouts: 6.26 us -> none  [transposed(): lax.dot_general(left, right, (((0,), (0,)), ((), ())), precision=HIGH, pr...]
  transfers between devices with their start and end apart: 5 -> 0, of which waited for: 4 -> 0; matrix products, arithmetic and copies ran while one was open for 12% -> 0% of each run, Pallas kernels for 0% -> 0%
where the time goes in v1:
time: 199 us; the launch traced here: 198 us
  Pallas kernels  192 us (96%)
  local copies, waits for them, and re-layouts  5.64 us (3%)
    pallas_call x1, Pallas kernels, shards(): pl.pallas_call(kernel, out_shape=(jax.ShapeDtypeStruct((GROUPS, m, cols),...  192 us
    reshape x2, local copies, waits for them, and re-layouts, shards(): return (fit.reshape(members, cols).T, infl.reshape(members, rows).T)  4.25 us

profile of v1, /device:TPU:0, one launch (start us, length us, event | category | flops | bytes accessed | tf_op | source)
XLA Modules:
  0.0 198.5 jit_solution(12856195226687045947)
XLA Ops:
  0.6 1.4 copy.7.step_size
  2.0 192.2 %shard_map.68 = (f32[2,64,5120]{2,1,0:T(8,128)}, f32[2,64,960]{2,1,0:T(8,128)}) custom-call(f32[960,5120]{1,0:T(8,128)} %design.1, f32[5120,128]{1,0:T(8,128)} %coef.1, s32[960,128]{1,0:T(8,128)} %counts.1, f32[1,960]{1,0:T(1,128)} %bitcast.10, f32[128,1]{1,0:T(8,128)} %copy.7.step_size), custom_call_target="tpu_custom_call" | custom-call | tf_op jit(solution)/shard_map/pallas_call | solution.py:380
  194.2 0.0 copy-start
  194.2 3.3 %copy.8 = f32[128,5120]{0,1:T(8,128)} copy(f32[128,5120]{1,0:T(8,128)} %bitcast.7) | data formatting | bytes 5242880 | tf_op jit(solution)/shard_map/reshape | solution.py:422
  197.5 0.0 copy-done
  197.5 1.0 copy.9
Async XLA Ops:
  194.2 3.3 %copy-start = (f32[2,64,960]{2,1,0:T(8,128)S(1)}, f32[2,64,960]{2,1,0:T(8,128)}, u32[]{:S(2)}) copy-start(f32[2,64,960]{2,1,0:T(8,128)} %get-tuple-element.5) | copy-start | bytes 1474564

commit v2 on v1

v2 whole, which is shorter than its diff:
```python
import functools

import jax
import jax.numpy as jnp
from jax import lax
from jax.experimental import pallas as pl
from jax.experimental.pallas import tpu as pltpu
from jax.sharding import PartitionSpec as P

STEPS = 3
SIDE = 4
LOADS = 10
GROUPS = 2
BLOCKS = (384, 256)
ORDER = (
    "AX3", "AG21", "AG11", "AG31", "BX2", "AG20", "AG01", "AG10", "AG30", "KKS0", "KKS1", "AP211", "AP201",
    "BX3", "BG20", "BG10", "BG30", "AG00", "AP210", "AP200", "BG21", "BG00", "BG11", "BG31", "KKR",
    "BP200", "BP210", "AP310", "AP300", "AP301", "AP311", "BG01", "BP201", "BP211", "BP310", "BP300",
    "AP410", "AP400", "AF00", "AP411", "BP301", "AP401", "BP311", "BP410", "AF01", "BP400", "BF00", "AF20",
    "AF10", "AF30", "AF21", "AF31", "BP401", "BP411", "AF11", "AX1", "BF01", "BF10", "BF30", "BF21",
    "BF11", "AX2", "BF31", "BF20", "BX1",
)
MESH = pl.DeviceIdType.MESH
F32 = jnp.float32
BF16 = jnp.bfloat16


def dot(a, b, ca=1, cb=0):
    return lax.dot_general(a, b, (((ca,), (cb,)), ((), ())), preferred_element_type=F32)


def far_first(n):
    return [k for k in (4, 5, 3, 2, 6, 1, 7) if k < n]


def parts(x):
    high = x.astype(BF16)
    return high, (x - high.astype(F32)).astype(BF16)


def kernel(
    design, coef, counts, targets, step_size, fit_out, inf_out,
    steps, raw, dh, dl, cin, kin, wt, wtb, acc, curve, icat,
    grad, fit, infl, pred, r1, s1, r2, r3, rate, c1, sc, c2,
    load_sem, in_sem, out_sem,
    p1s, p1r, p2s, p2r, p3s, p3r, p4s, p4r, x1s, x1r, x2s, x2r, k1s, k1r, k2s, k2r,
):
    rows, cols = raw.shape
    members = wt.shape[0]
    m = members // GROUPS
    quarter = cols // (2 * SIDE)
    half = cols // 2
    part = m // SIDE
    peers = lax.axis_size("basis")
    piece = m // peers
    row, me = lax.axis_index("row"), lax.axis_index("basis")
    y, z = row // SIDE, lax.rem(row, SIDE)

    def at_y(d):
        return (lax.rem(y + d, SIDE) * SIDE + z, me)

    def at_z(d):
        return (y * SIDE + lax.rem(z + d, SIDE), me)

    def at_b(k):
        return (row, lax.rem(me + k, peers))

    def major(h):
        return y + h * (z - y)

    def minor(h):
        return z + h * (y - z)

    def inside(b):
        return slice(sum(BLOCKS[:b]), sum(BLOCKS[: b + 1]))

    def columns(h, q, b=None):
        w = slice(0, quarter) if b is None else inside(b)
        return pl.ds(pl.multiple_of(h * half + q * quarter + w.start, 128), w.stop - w.start)

    def share_rows(h, d=0):
        return pl.ds(pl.multiple_of(lax.rem(minor(h) + d, SIDE) * part, 8), part)

    def piece_rows(k=0):
        return pl.ds(pl.multiple_of(lax.rem(me + k, peers) * piece, 8), piece)

    def remote(src, dst, send, recv, to):
        return pltpu.make_async_remote_copy(
            src_ref=src, dst_ref=dst, send_sem=send, recv_sem=recv, device_id=to, device_id_type=MESH
        )

    width = cols // LOADS

    def load(i):
        c = pl.ds(pl.multiple_of(i * width, 128), width)
        return pltpu.make_async_copy(design.at[:, c], raw.at[:, c], load_sem.at[i])

    coef_in = pltpu.make_async_copy(coef, cin, in_sem.at[0])
    counts_in = pltpu.make_async_copy(counts, kin, in_sem.at[1])
    counts_in.start()
    coef_in.start()
    for i in range(LOADS):
        load(i).start()

    barrier = pltpu.get_barrier_semaphore()
    for d in range(1, SIDE):
        pl.semaphore_signal(barrier, inc=1, device_id=at_y(d), device_id_type=MESH)
        pl.semaphore_signal(barrier, inc=1, device_id=at_z(d), device_id_type=MESH)
    for k in range(1, peers):
        pl.semaphore_signal(barrier, inc=1, device_id=at_b(k), device_id_type=MESH)

    def first(h, d):
        return (lax.rem(y + d * (1 - h), SIDE) * SIDE + lax.rem(z + d * h, SIDE), me)

    def second(h, d):
        return first(1 - h, d)

    def send1(g, h, d, b):
        c = columns(h, lax.rem(major(h) + d, SIDE), b)
        return remote(
            grad.at[g, :, c], r1.at[g, h, d - 1, :, inside(b)],
            p1s.at[g, h, d - 1, b], p1r.at[g, h, d - 1, b], first(h, d),
        )

    def send2(g, h, d, b):
        return remote(
            s1.at[g, h, share_rows(h, d), inside(b)], r2.at[g, h, d - 1, :, inside(b)],
            p2s.at[g, h, d - 1, b], p2r.at[g, h, d - 1, b], second(h, d),
        )

    def send3(g, h, d, b):
        mine = fit.at[g, share_rows(h), columns(h, major(h), b)]
        return remote(mine, mine, p3s.at[g, h, d - 1, b], p3r.at[g, h, d - 1, b], second(h, d))

    def send4(g, h, d, b):
        mine = fit.at[g, :, columns(h, major(h), b)]
        return remote(mine, mine, p4s.at[g, h, d - 1, b], p4r.at[g, h, d - 1, b], first(h, d))

    def sendx1(g, k):
        return remote(
            pred.at[g, piece_rows(k)], r3.at[g, k - 1], x1s.at[g, k - 1], x1r.at[g, k - 1], at_b(k)
        )

    def sendx2(g, k):
        mine = infl.at[g, piece_rows()]
        return remote(mine, mine, x2s.at[g, k - 1], x2r.at[g, k - 1], at_b(k))

    def sendk1(h, d):
        return remote(
            curve.at[:, columns(h, lax.rem(major(h) + d, SIDE))], c1.at[h, d - 1],
            k1s.at[h, d - 1], k1r.at[h, d - 1], first(h, d),
        )

    def sendk2(h, d):
        return remote(
            sc.at[h, :, share_rows(h, d)], c2.at[h, d - 1],
            k2s.at[h, d - 1], k2r.at[h, d - 1], second(h, d),
        )

    def gathered(g):
        for k in far_first(peers):
            sendx2(g, k).wait_recv()
        for k in far_first(peers):
            sendx2(g, k).wait_send()
        high, low = parts(infl[g])
        icat[g, 0:m] = high
        icat[g, m:] = low

    def gradients(g, d, b):
        def body(h, _):
            c = columns(h, lax.rem(major(h) + d, SIDE), b)
            both = dot(icat[g], dh[:, c])
            grad[g, :, c] = both[:m] + both[m:] + dot(icat[g, 0:m], dl[:, c])
            if d:
                send1(g, h, d, b).start()
            return 0

        lax.fori_loop(0, 2, body, 0)

    def reduce1(g, h, b):
        for d in range(1, SIDE):
            send1(g, h, d, b).wait_recv()
        w = inside(b)
        mine = grad[g, :, columns(h, major(h), b)]
        s1[g, h, :, w] = (mine + r1[g, h, 0, :, w]) + (r1[g, h, 1, :, w] + r1[g, h, 2, :, w])
        for d in (2, 1, 3):
            send2(g, h, d, b).start()

    def update(g, h, b):
        for d in range(1, SIDE):
            send2(g, h, d, b).wait_recv()
        w = inside(b)
        total = (s1[g, h, share_rows(h), w] + r2[g, h, 0, :, w]) + (r2[g, h, 1, :, w] + r2[g, h, 2, :, w])
        c = columns(h, major(h), b)
        fit[g, share_rows(h), c] = fit[g, share_rows(h), c] - total * rate[g, h, :, w]
        for d in (2, 1, 3):
            send3(g, h, d, b).start()
        for d in range(1, SIDE):
            send1(g, h, d, b).wait_send()

    def spread(g, h, b):
        for d in range(1, SIDE):
            send3(g, h, d, b).wait_recv()
        for d in (2, 1, 3):
            send4(g, h, d, b).start()
        for d in range(1, SIDE):
            send2(g, h, d, b).wait_send()

    def predict(g, d, b):
        if d == 0 and b == 0:
            pred[g] = jnp.zeros_like(pred[g])

        def body(h, _):
            if d:
                send4(g, h, d, b).wait_recv()
            c = columns(h, lax.rem(major(h) + SIDE - d, SIDE), b)
            high, low = parts(fit[g, :, c])
            both = dot(jnp.concatenate([high, low], 0), dh[:, c], 1, 1)
            pred[g] += both[:m] + both[m:] + dot(high, dl[:, c], 1, 1)
            return 0

        lax.fori_loop(0, 2, body, 0)

    def spread_sent(g):
        for h in range(2):
            for d in range(1, SIDE):
                for b in range(len(BLOCKS)):
                    send3(g, h, d, b).wait_send()
                    send4(g, h, d, b).wait_send()

    def scatter_pred(g):
        for k in far_first(peers):
            sendx1(g, k).start()

    def influence(g):
        for k in far_first(peers):
            sendx1(g, k).wait_recv()
        total = pred[g, piece_rows()]
        for k in range(1, peers):
            total = total + r3[g, k - 1]
        residual = total - targets[...]
        w = wt[pl.ds(pl.multiple_of(g * m + me * piece, 8), piece)]
        infl[g, piece_rows()] = w * residual / jnp.sqrt(1.0 + residual * residual)
        for k in far_first(peers):
            sendx2(g, k).start()
        for k in far_first(peers):
            sendx1(g, k).wait_send()

    steps[...] = jnp.broadcast_to(step_size[...], (members, members)).T
    counts_in.wait()
    wt[...] = kin[...].astype(F32).T
    wtb[...] = wt[...].astype(BF16)
    coef_in.wait()
    acc[...] = jnp.zeros_like(acc)

    def first_chunk(i, _):
        load(i).wait()
        c = pl.ds(pl.multiple_of(i * width, 128), width)
        high, low = parts(raw[:, c])
        dh[:, c] = high
        dl[:, c] = low
        fh, fl = parts(cin[c, :])
        both = dot(high, jnp.concatenate([fh, fl], 1))
        acc[...] += both[:, :members] + both[:, members:] + dot(low, fh)
        return 0

    lax.fori_loop(0, LOADS, first_chunk, 0)
    flipped = acc[...].T
    for g in range(GROUPS):
        pred[g] = flipped[g * m : (g + 1) * m]
    pl.semaphore_wait(barrier, 2 * (SIDE - 1) + peers - 1)
    for g in range(GROUPS):
        scatter_pred(g)

    def curve_part(d):
        def body(h, _):
            c = columns(h, lax.rem(major(h) + d, SIDE))
            x = raw[:, c]
            high, low = parts(x * x)
            curve[:, c] = dot(wtb[...], high) + dot(wtb[...], low)
            if d:
                sendk1(h, d).start()
            return 0

        lax.fori_loop(0, 2, body, 0)

    def curve_sum(h):
        for d in range(1, SIDE):
            sendk1(h, d).wait_recv()
        total = (curve[:, columns(h, major(h))] + c1[h, 0]) + (c1[h, 1] + c1[h, 2])
        for g in range(GROUPS):
            sc[h, g] = total[g * m : (g + 1) * m]
        for d in (2, 1, 3):
            sendk2(h, d).start()

    def curve_rate():
        for h in range(2):
            for d in range(1, SIDE):
                sendk2(h, d).wait_recv()
            for g in range(GROUPS):
                total = (sc[h, g, share_rows(h)] + c2[h, 0, g]) + (c2[h, 1, g] + c2[h, 2, g])
                mine = pl.ds(pl.multiple_of(g * m + minor(h) * part, 8), part)
                rate[g, h] = steps[mine, 0:1] / (total + 0.01)
        for h in range(2):
            for d in range(1, SIDE):
                sendk1(h, d).wait_send()
                sendk2(h, d).wait_send()

    curve_part(2)
    curve_part(1)
    influence(0)
    curve_part(3)
    curve_part(0)
    for h in range(2):
        start = pl.multiple_of(h * half + major(h) * quarter, 128)
        own = cin[pl.ds(start, quarter), :].T
        for g in range(GROUPS):
            fit[g, :, columns(h, major(h))] = own[g * m : (g + 1) * m]

    stages = dict(
        X3=gathered, G=gradients, P2=reduce1, P3=update, P4=spread, F=predict, KS=curve_sum, KR=curve_rate
    )

    def run(token):
        if token[0] == "K":
            name, where = token[1:3], token[3:]
            args = [int(v) for v in where]
        else:
            g = "AB".index(token[0])
            name = token[1:2] if token[1] in "GF" else token[1:3]
            args = [g] + [int(v) for v in token[1 + len(name) :]]
        if name == "X1":
            spread_sent(*args)
            scatter_pred(*args)
        elif name == "X2":
            influence(*args)
        else:
            stages[name](*args)

    turn = ORDER.index("BX3")

    def guard(i):
        token = ORDER[i]
        if token[0] == "K":
            return "first"
        if token[0] == "B" and i < turn:
            return "always" if token == "BX2" else "later"
        return "more" if token[1] == "F" or token[1:] in ("X1", "X2") else "always"

    def step(s, _):
        tests = dict(first=s == 0, later=s > 0, more=s < STEPS - 1)
        i = 0
        while i < len(ORDER):
            kind, j = guard(i), i
            while j < len(ORDER) and guard(j) == kind:
                j += 1

            def stretch(i=i, j=j):
                for token in ORDER[i:j]:
                    run(token)

            if kind == "always":
                stretch()
            else:
                pl.when(tests[kind])(stretch)
            i = j
        return 0

    lax.fori_loop(0, STEPS, step, 0)
    for token in ORDER[:turn]:
        if token[0] == "B" and token[1] in "GP":
            run(token)

    inf_copy = pltpu.make_async_copy(infl, inf_out, in_sem.at[0])
    inf_copy.start()

    def out_copy(g, h, d):
        c = columns(h, lax.rem(major(h) + SIDE - d, SIDE))
        return pltpu.make_async_copy(fit.at[g, :, c], fit_out.at[g, :, c], out_sem.at[g, h, d])

    for g in range(GROUPS):
        for h in range(2):
            out_copy(g, h, 0).start()
            for d in range(1, SIDE):
                for b in range(len(BLOCKS)):
                    send4(g, h, d, b).wait_recv()
                out_copy(g, h, d).start()
    for g in range(GROUPS):
        spread_sent(g)
        for h in range(2):
            for d in range(SIDE):
                out_copy(g, h, d).wait()
    inf_copy.wait()


def shards(design, targets, counts, coefficients, step_size):
    rows, cols = design.shape
    members = coefficients.shape[1]
    m = members // GROUPS
    quarter = cols // (2 * SIDE)
    part = m // SIDE
    peers = lax.axis_size("basis")
    piece = m // peers
    vmem = pltpu.VMEM
    dma = pltpu.SemaphoreType.DMA
    gh = (GROUPS, 2, SIDE - 1)
    ghb = (*gh, len(BLOCKS))
    any_spec = pl.BlockSpec(memory_space=pl.ANY)
    vmem_spec = pl.BlockSpec(memory_space=pltpu.VMEM)
    fit, infl = pl.pallas_call(
        kernel,
        out_shape=(
            jax.ShapeDtypeStruct((GROUPS, m, cols), F32),
            jax.ShapeDtypeStruct((GROUPS, m, rows), F32),
        ),
        in_specs=[any_spec, any_spec, any_spec, vmem_spec, vmem_spec],
        out_specs=(any_spec, any_spec),
        scratch_shapes=[
            vmem((members, members), F32),
            vmem((rows, cols), F32),
            vmem((rows, cols), BF16),
            vmem((rows, cols), BF16),
            vmem((cols, members), F32),
            vmem((rows, members), jnp.int32),
            vmem((members, rows), F32),
            vmem((members, rows), BF16),
            vmem((rows, members), F32),
            vmem((members, cols), F32),
            vmem((GROUPS, 2 * m, rows), BF16),
            vmem((GROUPS, m, cols), F32),
            vmem((GROUPS, m, cols), F32),
            vmem((GROUPS, m, rows), F32),
            vmem((GROUPS, m, rows), F32),
            vmem((*gh, m, quarter), F32),
            vmem((GROUPS, 2, m, quarter), F32),
            vmem((*gh, part, quarter), F32),
            vmem((GROUPS, peers - 1, piece, rows), F32),
            vmem((GROUPS, 2, part, quarter), F32),
            vmem((2, SIDE - 1, members, quarter), F32),
            vmem((2, GROUPS, m, quarter), F32),
            vmem((2, SIDE - 1, GROUPS, part, quarter), F32),
            dma((LOADS,)),
            dma((2,)),
            dma((GROUPS, 2, SIDE)),
            *[dma(ghb) for _ in range(8)],
            *[dma((GROUPS, peers - 1)) for _ in range(4)],
            *[dma((2, SIDE - 1)) for _ in range(4)],
        ],
        compiler_params=pltpu.CompilerParams(
            collective_id=0, has_side_effects=True, vmem_limit_bytes=60 * 2**20
        ),
    )(design, coefficients, counts, targets[None, :], step_size[None, :])
    return fit.reshape(members, cols).T, infl.reshape(members, rows).T


def solution(mesh):
    return jax.shard_map(
        shards,
        mesh=mesh,
        in_specs=(P("row", "basis"), P("row"), P("row", None), P("basis", None), P()),
        out_specs=(P("basis", None), P("row", None)),
        check_vma=False,
    )
```

time: 199 us -> 178 us (0.89)
  Pallas kernels: 192 us -> 173 us
    pallas_call x1, Pallas kernels: 192 us -> 173 us  [shards(): pl.pallas_call(kernel, out_shape=(jax.ShapeDtypeStruct((GROUPS, m, cols),...]
where the time goes in v2:
time: 178 us; the launch traced here: 177 us
  Pallas kernels  173 us (97%)
  local copies, waits for them, and re-layouts  4.25 us (2%)
    pallas_call x1, Pallas kernels, shards(): pl.pallas_call(kernel, out_shape=(jax.ShapeDtypeStruct((GROUPS, m, cols),...  173 us
    reshape x2, local copies, waits for them, and re-layouts, shards(): return (fit.reshape(members, cols).T, infl.reshape(members, rows).T)  4.25 us

profile of v2, /device:TPU:0, one launch (start us, length us, event | category | flops | bytes accessed | tf_op | source)
XLA Modules:
  0.0 177.5 jit_solution(10663940328943771857)
XLA Ops:
  0.6 172.6 %shard_map.68 = (f32[2,64,5120]{2,1,0:T(8,128)}, f32[2,64,960]{2,1,0:T(8,128)}) custom-call(f32[960,5120]{1,0:T(8,128)} %design.1, f32[5120,128]{1,0:T(8,128)} %coef.1, s32[960,128]{1,0:T(8,128)} %counts.1, f32[1,960]{1,0:T(1,128)} %bitcast.10, f32[1,128]{1,0:T(1,128)} %bitcast.11), custom_call_target="tpu_custom_call" | custom-call | tf_op jit(solution)/shard_map/pallas_call | solution.py:410
  173.2 0.0 copy-start
  173.2 3.3 %copy.7 = f32[128,5120]{0,1:T(8,128)} copy(f32[128,5120]{1,0:T(8,128)} %bitcast.7) | data formatting | bytes 5242880 | tf_op jit(solution)/shard_map/reshape | solution.py:453
  176.5 0.0 copy-done
  176.5 1.0 copy.8
Async XLA Ops:
  173.2 3.3 %copy-start = (f32[2,64,960]{2,1,0:T(8,128)S(1)}, f32[2,64,960]{2,1,0:T(8,128)}, u32[]{:S(2)}) copy-start(f32[2,64,960]{2,1,0:T(8,128)} %get-tuple-element.5) | copy-start | bytes 1474564

commit v3 on v2

--- a/solution.py
+++ b/solution.py
@@ -9,9 +9,9 @@
 
 STEPS = 3
 SIDE = 4
-LOADS = 10
+LOADS = 8
 GROUPS = 2
-BLOCKS = (384, 256)
+BLOCKS = (256, 384)
 ORDER = (
     "AX3", "AG21", "AG11", "AG31", "BX2", "AG20", "AG01", "AG10", "AG30", "KKS0", "KKS1", "AP211", "AP201",
     "BX3", "BG20", "BG10", "BG30", "AG00", "AP210", "AP200", "BG21", "BG00", "BG11", "BG31", "KKR",
@@ -330,8 +330,8 @@
             name = token[1:2] if token[1] in "GF" else token[1:3]
             args = [g] + [int(v) for v in token[1 + len(name) :]]
         if name == "X1":
+            scatter_pred(*args)
             spread_sent(*args)
-            scatter_pred(*args)
         elif name == "X2":
             influence(*args)
         else:

time: 178 us -> 178 us (level)
  no operation moved by 1% of the time
where the time goes in v3:
time: 178 us; the launch traced here: 177 us
  Pallas kernels  172 us (97%)
  local copies, waits for them, and re-layouts  4.25 us (2%)
    pallas_call x1, Pallas kernels, shards(): pl.pallas_call(kernel, out_shape=(jax.ShapeDtypeStruct((GROUPS, m, cols),...  172 us
    reshape x2, local copies, waits for them, and re-layouts, shards(): return (fit.reshape(members, cols).T, infl.reshape(members, rows).T)  4.25 us

profile of v3, /device:TPU:0, one launch (start us, length us, event | category | flops | bytes accessed | tf_op | source)
XLA Modules:
  0.0 177.4 jit_solution(11753776648923889483)
XLA Ops:
  0.6 172.5 %shard_map.68 = (f32[2,64,5120]{2,1,0:T(8,128)}, f32[2,64,960]{2,1,0:T(8,128)}) custom-call(f32[960,5120]{1,0:T(8,128)} %design.1, f32[5120,128]{1,0:T(8,128)} %coef.1, s32[960,128]{1,0:T(8,128)} %counts.1, f32[1,960]{1,0:T(1,128)} %bitcast.10, f32[1,128]{1,0:T(1,128)} %bitcast.11), custom_call_target="tpu_custom_call" | custom-call | tf_op jit(solution)/shard_map/pallas_call | solution.py:410
  173.1 0.0 copy-start
  173.1 3.3 %copy.7 = f32[128,5120]{0,1:T(8,128)} copy(f32[128,5120]{1,0:T(8,128)} %bitcast.7) | data formatting | bytes 5242880 | tf_op jit(solution)/shard_map/reshape | solution.py:453
  176.4 0.0 copy-done
  176.4 1.0 copy.8
Async XLA Ops:
  173.1 3.3 %copy-start = (f32[2,64,960]{2,1,0:T(8,128)S(1)}, f32[2,64,960]{2,1,0:T(8,128)}, u32[]{:S(2)}) copy-start(f32[2,64,960]{2,1,0:T(8,128)} %get-tuple-element.5) | copy-start | bytes 1474564
